TPU v7x, 128 devices: a whole 4x4x4 slice. The times are simulated.
128 devices in a mesh: lag: 8 (over y, core), col: 16 (over z, x).
Axes of the slice: x: 4, y: 4, z: 4, core: 2. Of those that a mesh axis runs over, the one named last changes fastest.
Arguments:
- lag_matrices: float32 [128, 2048, 2048], P('lag', None, 'col'), may hold values from -0.03125 to 0.03125
- history: float32 [128, 2048, 256], P('lag', 'col'), may hold values from -6 to 6
- excitation: float32 [4, 2048, 256], P(None, 'col'), may hold values from -6 to 6
Outputs:
- densities: float32 [4, 2048, 256], P(None, 'col')
All inputs are finite; a program needn't handle non-finite values.
Results may differ from a plain program's by a relative error of at most 0.0001.
Values sent between devices are 32-bit elements; how exact they have to be, the bound alone decides.
A program may use at most 64 MiB of HBM per device.

v0:
```python
import jax
import jax.numpy as jnp
from jax import lax
from jax.sharding import PartitionSpec as P


def passed_along(value, axis, steps):
    count = lax.axis_size(axis)
    first, last = (max(0, -steps), min(count, count - steps))
    return lax.ppermute(value, axis, [(source, source + steps) for source in range(first, last)])


def in_blocks(value, dim, size):
    before, after = (value.shape[:dim], value.shape[dim + 1 :])
    return jnp.moveaxis(value.reshape(*before, size, -1, *after), dim, 0)


def summed_on_arrival(value, axis, dim):
    pieces = in_blocks(value, dim, lax.axis_size(axis))
    arrived = lax.all_to_all(pieces, axis, split_axis=0, concat_axis=0, tiled=True)
    return arrived.sum(axis=0)


def sent_to_all(value, axis):
    copies = jnp.broadcast_to(value, (lax.axis_size(axis), *value.shape))
    return lax.all_to_all(copies, axis, split_axis=0, concat_axis=0, tiled=True)


def of_everyone(value, axis):
    return sent_to_all(value, axis).sum(axis=0)


def apply_lags(matrices, sources):
    return jnp.einsum("jab,jbs->as", matrices, sources, precision=lax.Precision.HIGHEST)


def local(lag_matrices, history, excitation):
    lag_count = lag_matrices.shape[0]
    block_rows = lag_matrices.shape[2]
    total_steps = excitation.shape[0]
    back_steps = total_steps - 1
    owner_index = lax.axis_index("lag")
    is_head = (owner_index == 0).astype(jnp.float32)
    carried = passed_along(history[lag_count - back_steps :], "lag", 1)
    blank = jnp.zeros_like(history[0])
    newest = []
    for moment in range(total_steps):
        pre_new = jnp.stack(
            [
                newest[back_steps - 1 - offset] if back_steps - 1 - offset < moment else blank
                for offset in range(back_steps)
            ]
        )
        extended = jnp.concatenate([carried + is_head * pre_new, history], axis=0)
        sources = extended[back_steps - moment : back_steps - moment + lag_count]

        def step_term(row_start, row_count, sources=sources):
            return apply_lags(lag_matrices, sources)

        summed = summed_on_arrival(
            step_term(jnp.int32(0), block_rows * lax.axis_size("col")), "col", 0
        )
        summed = of_everyone(summed, "lag")
        newest.append(excitation[moment] - summed)
    return jnp.stack(newest)


def solution(mesh):
    return jax.shard_map(
        local,
        mesh=mesh,
        in_specs=(P("lag", None, "col"), P("lag", "col", None), P(None, "col", None)),
        out_specs=P(None, "col", None),
        check_vma=False,
    )
```

profile of v0, /device:TPU:1, one launch (start us, length us, event | category | flops | bytes accessed | tf_op | source)
XLA Modules:
  0.0 297.5 jit_solution(7014659102211961555)
XLA Ops:
  0.0 16.3 %fusion.17 = f32[2048,256,1]{1,0,2:T(8,128)S(1)} fusion(f32[16,2048,128]{2,1,0:T(8,128)} %param.3, f32[16,128,256]{2,1,0:T(8,128)} %param.4), kind=kOutput, calls=%fused_computation.33 | convolution fusion | flops 12884901888 | bytes 20971520 | tf_op jit(solution)/shard_map/jab,jbs->as/dot_general | solution.py:34
  16.3 35.5 %all_to_all.40 = f32[16,128,256]{2,1,0:T(8,128)S(1)} all-to-all(f32[16,128,256]{2,1,0:T(8,128)S(1)} %bitcast.41), channel_id=1, replica_groups=mesh['lag'=8,'col'=16] {'col'}, dimensions={0} | all-to-all | bytes 4194304 | tf_op jit(solution)/shard_map/all_to_all | solution.py:20
  51.8 0.1 reduce_sum.80
  51.9 1.1 broadcast_in_dim.12
  53.0 6.5 %all-to-all-start.1 = ((f32[8,128,256]{2,1,0:T(8,128)}), f32[8,128,256]{2,1,0:T(8,128)S(1)}, u32[]{:S(2)}, u32[]{:S(2)}) async-start(f32[8,128,256]{2,1,0:T(8,128)} %broadcast_in_dim.12), calls=%async_computation.1 | async-start | bytes 2097152 | tf_op jit(solution)/shard_map/all_to_all | solution.py:26
  59.5 1.9 copy.34
  61.4 0.8 slice.32
  62.2 3.5 %collective-permute-start = (f32[3,128,256]{1,2,0:T(8,128)}, f32[3,128,256]{1,2,0:T(8,128)S(1)}, u32[]{:S(2)}, u32[]{:S(2)}) collective-permute-start(f32[3,128,256]{1,2,0:T(8,128)} %slice.32), channel_id=1, source_target_pairs={{0,16},{16,32},{32,48},{48,64},{64,80},{80,96},{96,112},{1,17},{17... | collective-permute-start | bytes 1179656 | tf_op jit(solution)/shard_map/ppermute | solution.py:10
  65.7 1.9 fusion.16
  67.6 1.6 copy.56
  69.3 5.2 %all-to-all-done.1 = f32[8,128,256]{2,1,0:T(8,128)S(1)} async-done(((f32[8,128,256]{2,1,0:T(8,128)}), f32[8,128,256]{2,1,0:T(8,128)S(1)}, u32[]{:S(2)}, u32[]{:S(2)}) %all-to-all-start.1) | async-done | bytes 1048608 | tf_op jit(solution)/shard_map/all_to_all | solution.py:26
  74.5 0.7 reduce_sum.81
  75.2 1.0 copy.32
  76.2 0.9 bitcast_subtract_fusion.3
  77.1 0.0 copy-start
  77.1 0.0 collective-permute-done
  77.2 17.0 %fusion.8 = f32[32,16,8,128]{3,2,1,0:T(8,128)S(1)} fusion(f32[16,2048,128]{2,1,0:T(8,128)} %param.3, f32[16,128,256]{1,2,0:T(8,128)S(1)} %copy.34, f32[3,128,256]{1,2,0:T(8,128)S(1)} %multiply_add_fusion), kind=kOutput, calls=%fused_computation.14 | convolution fusion | flops 12885524480 | bytes 21364736 | tf_op jit(solution)/shard_map/jab,jbs->as/dot_general | solution.py:34
  94.2 0.0 copy-done
  94.2 0.2 copy.68
  94.4 30.4 %all_to_all.41 = f32[16,128,256]{1,2,0:T(8,128)} all-to-all(f32[16,128,256]{1,2,0:T(8,128)S(1)} %bitcast.42), channel_id=1, replica_groups=mesh['lag'=8,'col'=16] {'col'}, dimensions={0} | all-to-all | bytes 4194304 | tf_op jit(solution)/shard_map/all_to_all | solution.py:20
  124.8 1.7 reduce_sum.83
  126.5 0.1 copy.38
  126.6 1.1 broadcast_in_dim.13
  127.7 5.8 %all-to-all-start.3 = ((f32[8,128,256]{2,1,0:T(8,128)}), f32[8,128,256]{2,1,0:T(8,128)S(1)}, u32[]{:S(2)}, u32[]{:S(2)}) async-start(f32[8,128,256]{2,1,0:T(8,128)} %broadcast_in_dim.13), calls=%async_computation.3 | async-start | bytes 2097152 | tf_op jit(solution)/shard_map/all_to_all | solution.py:26
  133.5 1.7 copy.57
  135.2 13.3 %all-to-all-done.3 = f32[8,128,256]{2,1,0:T(8,128)S(1)} async-done(((f32[8,128,256]{2,1,0:T(8,128)}), f32[8,128,256]{2,1,0:T(8,128)S(1)}, u32[]{:S(2)}, u32[]{:S(2)}) %all-to-all-start.3) | async-done | bytes 1048608 | tf_op jit(solution)/shard_map/all_to_all | solution.py:26
  148.5 0.7 reduce_sum.84
  149.2 1.0 copy.39
  150.2 0.9 bitcast_subtract_fusion.2
  151.1 0.0 copy-start.2
  151.2 1.1 fusion.10
  152.2 17.0 %fusion.7 = f32[32,16,8,128]{3,2,1,0:T(8,128)S(1)} fusion(f32[16,2048,128]{2,1,0:T(8,128)} %param.3, f32[16,128,256]{1,2,0:T(8,128)S(1)} %copy.34, f32[3,128,256]{1,2,0:T(8,128)S(1)} %fusion.10), kind=kOutput, calls=%fused_computation.13 | convolution fusion | flops 12885524480 | bytes 21364736 | tf_op jit(solution)/shard_map/jab,jbs->as/dot_general | solution.py:34
  169.3 0.0 copy-done.2
  169.3 0.2 copy.67
  169.5 30.6 %all_to_all.42 = f32[16,128,256]{1,2,0:T(8,128)} all-to-all(f32[16,128,256]{1,2,0:T(8,128)S(1)} %bitcast.43), channel_id=1, replica_groups=mesh['lag'=8,'col'=16] {'col'}, dimensions={0} | all-to-all | bytes 4194304 | tf_op jit(solution)/shard_map/all_to_all | solution.py:20
  200.1 1.7 reduce_sum.86
  201.8 0.1 copy.44
  201.9 1.1 broadcast_in_dim.14
  203.0 5.5 %all-to-all-start.5 = ((f32[8,128,256]{2,1,0:T(8,128)}), f32[8,128,256]{2,1,0:T(8,128)S(1)}, u32[]{:S(2)}, u32[]{:S(2)}) async-start(f32[8,128,256]{2,1,0:T(8,128)} %broadcast_in_dim.14), calls=%async_computation.5 | async-start | bytes 2097152 | tf_op jit(solution)/shard_map/all_to_all | solution.py:26
  208.5 1.6 copy.58
  210.1 13.3 %all-to-all-done.5 = f32[8,128,256]{2,1,0:T(8,128)S(1)} async-done(((f32[8,128,256]{2,1,0:T(8,128)}), f32[8,128,256]{2,1,0:T(8,128)S(1)}, u32[]{:S(2)}, u32[]{:S(2)}) %all-to-all-start.5) | async-done | bytes 1048608 | tf_op jit(solution)/shard_map/all_to_all | solution.py:26
  223.5 0.7 reduce_sum.87
  224.2 1.0 copy.45
  225.2 0.9 bitcast_subtract_fusion.1
  226.1 1.0 fusion.12
  227.1 17.0 %fusion.6 = f32[32,16,8,128]{3,2,1,0:T(8,128)S(1)} fusion(f32[16,2048,128]{2,1,0:T(8,128)} %param.3, f32[16,128,256]{1,2,0:T(8,128)S(1)} %copy.34, f32[3,128,256]{1,2,0:T(8,128)S(1)} %fusion.12), kind=kOutput, calls=%fused_computation.12 | convolution fusion | flops 12885524480 | bytes 21364736 | tf_op jit(solution)/shard_map/jab,jbs->as/dot_general | solution.py:34
  244.2 0.2 copy.66
  244.4 30.0 %all_to_all.43 = f32[16,128,256]{1,2,0:T(8,128)S(1)} all-to-all(f32[16,128,256]{1,2,0:T(8,128)S(1)} %bitcast.44), channel_id=1, replica_groups=mesh['lag'=8,'col'=16] {'col'}, dimensions={0} | all-to-all | bytes 4194304 | tf_op jit(solution)/shard_map/all_to_all | solution.py:20
  274.3 0.1 reduce_sum.89
  274.4 0.0 copy-start.4
  274.5 0.1 copy.50
  274.6 1.1 broadcast_in_dim.15
  275.6 0.0 copy-start.1
  275.6 0.0 copy-start.3
  275.6 5.6 %all-to-all-start.7 = ((f32[8,128,256]{2,1,0:T(8,128)}), f32[8,128,256]{2,1,0:T(8,128)S(1)}, u32[]{:S(2)}, u32[]{:S(2)}) async-start(f32[8,128,256]{2,1,0:T(8,128)} %broadcast_in_dim.15), calls=%async_computation.7 | async-start | bytes 2097152 | tf_op jit(solution)/shard_map/all_to_all | solution.py:26
  281.3 0.0 copy-done.4
  281.3 0.1 copy.59
  281.4 14.9 %all-to-all-done.7 = f32[8,128,256]{2,1,0:T(8,128)S(1)} async-done(((f32[8,128,256]{2,1,0:T(8,128)}), f32[8,128,256]{2,1,0:T(8,128)S(1)}, u32[]{:S(2)}, u32[]{:S(2)}) %all-to-all-start.7) | async-done | bytes 1048608 | tf_op jit(solution)/shard_map/all_to_all | solution.py:26
  296.3 0.1 reduce_sum.90
  296.4 0.1 copy.51
  296.5 0.0 copy-done.1
  296.5 0.0 copy-done.3
  296.5 1.0 copy.52
  (4 shorter events, 0.1 us)
Async XLA Ops:
  53.0 21.5 %all-to-all-start.1 = ((f32[8,128,256]{2,1,0:T(8,128)}), f32[8,128,256]{2,1,0:T(8,128)S(1)}, u32[]{:S(2)}, u32[]{:S(2)}) async-start(f32[8,128,256]{2,1,0:T(8,128)} %broadcast_in_dim.12), calls=%async_computation.1 | async-start | bytes 2097152 | tf_op jit(solution)/shard_map/all_to_all | solution.py:26
  62.2 14.9 %collective-permute-start = (f32[3,128,256]{1,2,0:T(8,128)}, f32[3,128,256]{1,2,0:T(8,128)S(1)}, u32[]{:S(2)}, u32[]{:S(2)}) collective-permute-start(f32[3,128,256]{1,2,0:T(8,128)} %slice.32), channel_id=1, source_target_pairs={{0,16},{16,32},{32,48},{48,64},{64,80},{80,96},{96,112},{1,17},{17... | collective-permute-start | bytes 1179656 | tf_op jit(solution)/shard_map/ppermute | solution.py:10
  77.1 17.1 %copy-start = (f32[1,128,256]{1,2,0:T(8,128)}, f32[1,128,256]{1,2,0:T(8,128)S(1)}, u32[]{:S(2)}) copy-start(f32[1,128,256]{1,2,0:T(8,128)S(1)} %bitcast_subtract_fusion.3) | copy-start | bytes 393220
  127.7 20.8 %all-to-all-start.3 = ((f32[8,128,256]{2,1,0:T(8,128)}), f32[8,128,256]{2,1,0:T(8,128)S(1)}, u32[]{:S(2)}, u32[]{:S(2)}) async-start(f32[8,128,256]{2,1,0:T(8,128)} %broadcast_in_dim.13), calls=%async_computation.3 | async-start | bytes 2097152 | tf_op jit(solution)/shard_map/all_to_all | solution.py:26
  151.1 18.1 %copy-start.2 = (f32[1,128,256]{1,2,0:T(8,128)}, f32[1,128,256]{1,2,0:T(8,128)S(1)}, u32[]{:S(2)}) copy-start(f32[1,128,256]{1,2,0:T(8,128)S(1)} %bitcast_subtract_fusion.2) | copy-start | bytes 393220
  203.0 20.5 %all-to-all-start.5 = ((f32[8,128,256]{2,1,0:T(8,128)}), f32[8,128,256]{2,1,0:T(8,128)S(1)}, u32[]{:S(2)}, u32[]{:S(2)}) async-start(f32[8,128,256]{2,1,0:T(8,128)} %broadcast_in_dim.14), calls=%async_computation.5 | async-start | bytes 2097152 | tf_op jit(solution)/shard_map/all_to_all | solution.py:26
  274.4 6.8 %copy-start.4 = (f32[1,128,256]{2,1,0:T(8,128)S(1)}, f32[1,128,256]{2,1,0:T(8,128)}, u32[]{:S(2)}) copy-start(f32[1,128,256]{2,1,0:T(8,128)} %get-tuple-element.8) | copy-start | bytes 393220
  275.6 20.8 %copy-start.1 = (f32[1,128,256]{1,2,0:T(8,128)S(1)}, f32[1,128,256]{1,2,0:T(8,128)}, u32[]{:S(2)}) copy-start(f32[1,128,256]{1,2,0:T(8,128)} %copy-done) | copy-start | bytes 393220
  275.6 20.8 %copy-start.3 = (f32[1,128,256]{1,2,0:T(8,128)S(1)}, f32[1,128,256]{1,2,0:T(8,128)}, u32[]{:S(2)}) copy-start(f32[1,128,256]{1,2,0:T(8,128)} %copy-done.2) | copy-start | bytes 393220
  275.6 20.6 %all-to-all-start.7 = ((f32[8,128,256]{2,1,0:T(8,128)}), f32[8,128,256]{2,1,0:T(8,128)S(1)}, u32[]{:S(2)}, u32[]{:S(2)}) async-start(f32[8,128,256]{2,1,0:T(8,128)} %broadcast_in_dim.15), calls=%async_computation.7 | async-start | bytes 2097152 | tf_op jit(solution)/shard_map/all_to_all | solution.py:26
where the time goes:
time: 298 us
  blocking collectives  126 us (42%)
  matrix products  67.4 us (23%)
  waiting for transfers between devices  46.8 us (16%)
  starting transfers between devices  27 us (9%)
  local copies, waits for them, and re-layouts  18.9 us (6%)
  other arithmetic  10.8 us (4%)
    all_to_all x4, blocking collectives, summed_on_arrival(): lax.all_to_all(pieces, axis, split_axis=0, concat_axis=0, tiled=True)  126 us
    dot_general x4, matrix products, apply_lags(): jnp.einsum('jab,jbs->as', matrices, sources, precision=lax.Precision.HIGH...  67.4 us
    all_to_all x4, waiting for transfers between devices, sent_to_all(): return lax.all_to_all(copies, axis, split_axis=0, concat_axis=0, tiled=True)  46.8 us
    all_to_all x4, starting transfers between devices, sent_to_all(): return lax.all_to_all(copies, axis, split_axis=0, concat_axis=0, tiled=True)  23.5 us
    unnamed x15, local copies, waits for them, and re-layouts  6.97 us
  transfers between devices with their start and end apart: 5, of which 4 were waited for; matrix products, arithmetic and copies ran while one was open for 4% of the time, Pallas kernels for 0%

commit v1 on v0

v1 whole, which is shorter than its diff:
```python
import jax
import jax.numpy as jnp
from jax import lax
from jax.experimental import pallas as pl
from jax.experimental.pallas import tpu as pltpu
from jax.sharding import PartitionSpec as P

MESH = pl.DeviceIdType.MESH
bf, f32 = jnp.bfloat16, jnp.float32

RING = 4
SLOTS = 8
SUB = 3
LAG_EXCH, LAG_ONE, LAG_TWO, LAG_THREE = 2, 3, 3, 3
LAG_GATHER, LAG_SCATTER = 3, 5


def halves(value):
    high = value.astype(bf)
    return high, (value - high.astype(f32)).astype(bf)


def dot(a, b):
    return jnp.dot(a, b, preferred_element_type=f32)


def kernel(
    a_ref, h_ref, e_ref, o_ref,
    mats, ext, xh, xl, both, first, part, swap,
    in1, sum1, in2, sum2, in3, total,
    near, near_b, terms, in_t, new, new_b, exc,
    s_mat, s_loc, s_carry, r_carry, s_near, r_near, s_fwd, r_fwd,
    s_swap, r_swap, s1, r1, s2, r2, s3, r3, s_t, r_t, s_g, r_g, s_o, r_o,
):
    lag, col = lax.axis_index("lag"), lax.axis_index("col")
    y, k = lag // 2, lag % 2
    z, x = col // RING, col % RING
    pos = {"x": x, "y": y, "z": z}
    other = 1 - k

    def device(**moved):
        at = {**pos, "k": k, **moved}
        return (at["y"] * 2 + at["k"], at["z"] * RING + at["x"])

    def turned(axis, steps):
        return lax.rem(pos[axis] + steps, RING)

    def send(src, dst, s_sem, r_sem, target):
        pltpu.make_async_remote_copy(
            src_ref=src, dst_ref=dst, send_sem=s_sem, recv_sem=r_sem,
            device_id=target, device_id_type=MESH,
        ).start()

    def await_bytes(ref, sem):
        pltpu.make_async_copy(ref, ref, sem).wait()

    load_h = pltpu.make_async_copy(h_ref, ext.at[pl.ds(3, 16)], s_loc.at[0])
    load_h.start()
    load_a = [
        pltpu.make_async_copy(a_ref.at[:, :, :, pl.ds(8 * t, 8)], mats.at[t], s_mat.at[t])
        for t in range(4)
    ]
    load_a[0].start()
    load_e = pltpu.make_async_copy(e_ref, exc, s_loc.at[1])
    load_e.start()
    for t in range(1, 4):
        load_a[t].start()

    barrier = pltpu.get_barrier_semaphore()
    cross = (lax.rem(y + jnp.where(k == 1, 1, RING - 1), RING) * 2 + other, col)
    peers = [device(k=other), cross]
    peers += [device(y=turned("y", d)) for d in range(1, RING)]
    peers += [
        device(z=turned("z", dz), x=turned("x", dx))
        for dz in range(RING) for dx in range(RING) if dz or dx
    ]
    for peer in peers:
        pl.semaphore_signal(barrier, inc=1, device_id=peer, device_id_type=MESH)

    @pl.when(lag == 0)
    def _():
        ext[0:3] = jnp.zeros((3, 128, 256), f32)

    load_h.wait()

    def set_block(kind, u):
        base = ext[1 + 2 * u]
        value = (base, ext[2 + 2 * u] - base, ext[2 * u] - base)[kind]
        rows = pl.ds(u * 128, 128)
        xh[kind, rows], xl[kind, rows] = halves(value)

    pl.semaphore_wait(barrier, len(peers))

    @pl.when(lag < 7)
    def _():
        after = (lag + 1, col)
        send(h_ref.at[15], ext.at[2], s_carry.at[0], r_carry.at[0], after)
        send(h_ref.at[pl.ds(13, 2)], ext.at[pl.ds(0, 2)], s_carry.at[1], r_carry.at[1], after)

    @pl.when(lag == 0)
    def _():
        pltpu.make_async_copy(a_ref.at[pl.ds(0, 3), :, 0], near, s_loc.at[2]).start()
        for j in range(3):
            for d in (1, 3, 2):
                send(a_ref.at[j, :, d], near.at[j], s_near, r_near, device(y=d))

    for u in range(2, 9):
        for kind in range(3):
            set_block(kind, u)
    for kind in range(2):
        set_block(kind, 1)

    events = {}

    def at(time, act):
        events.setdefault(time, []).append(act)

    def swap_send(s, n):
        send(part.at[s, n, other], swap.at[s, n], s_swap, r_swap.at[s, n], device(k=other))

    orders = (("x", "y", "z"), ("y", "z", "x"), ("z", "x", "y"))
    MEMORY = ("z", "x", "y")

    def block(ref, lead, axes, axis, index):
        return ref.at[(*lead, *(index if name == axis else slice(None) for name in axes))]

    def exchange(s, n):
        await_bytes(swap.at[s, n], r_swap.at[s, n])
        part[s, n, k] += swap[s, n]
        axis = orders[(2 * s + n) % 3][0]
        for d in (2, 1, 3):
            to = turned(axis, d)
            send(
                block(part, (s, n, k), MEMORY, axis, to), in1.at[s, n, d - 1],
                s1, r1.at[s, n], device(**{axis: to}),
            )

    def one(s, n):
        order = orders[(2 * s + n) % 3]
        left = tuple(name for name in MEMORY if name != order[0])
        await_bytes(in1.at[s, n], r1.at[s, n])
        mine = block(part, (s, n, k), MEMORY, order[0], pos[order[0]])[...]
        sum1[s, n] = (mine + in1[s, n, 0]) + (in1[s, n, 1] + in1[s, n, 2])
        for d in (2, 1, 3):
            to = turned(order[1], d)
            send(
                block(sum1, (s, n), left, order[1], to), in2.at[s, n, d - 1],
                s2, r2.at[s, n], device(**{order[1]: to}),
            )

    def two(s, n):
        order = orders[(2 * s + n) % 3]
        left = tuple(name for name in MEMORY if name != order[0])
        await_bytes(in2.at[s, n], r2.at[s, n])
        mine = block(sum1, (s, n), left, order[1], pos[order[1]])[...]
        sum2[s, n] = (mine + in2[s, n, 0]) + (in2[s, n, 1] + in2[s, n, 2])
        for d in (2, 1, 3):
            to = turned(order[2], d)
            send(
                sum2.at[s, n, to], in3.at[s, n, d - 1],
                s3, r3.at[s, n], device(**{order[2]: to}),
            )

    def three(s, n):
        order = orders[(2 * s + n) % 3]
        await_bytes(in3.at[s, n], r3.at[s, n])
        mine = sum2[s, n, pos[order[2]]]
        total[2 * (s // 4) + n, s % 4] = (mine + in3[s, n, 0]) + (in3[s, n, 1] + in3[s, n, 2])

    for s in range(SLOTS):
        for n in range(2):
            time = SUB * s + 1 + n
            at(time, lambda s=s, n=n: swap_send(s, n))
            at(time + LAG_EXCH, lambda s=s, n=n: exchange(s, n))
            at(time + LAG_EXCH + LAG_ONE, lambda s=s, n=n: one(s, n))
            at(time + LAG_EXCH + LAG_ONE + LAG_TWO, lambda s=s, n=n: two(s, n))
            at(time + LAG_EXCH + LAG_ONE + LAG_TWO + LAG_THREE, lambda s=s, n=n: three(s, n))

    def near_pass():
        @pl.when(k == 0)
        def _():
            @pl.when(y == 0)
            def _():
                pltpu.make_async_copy(a_ref.at[pl.ds(0, 3), :, 0], near, s_loc.at[2]).wait()

            @pl.when(y > 0)
            def _():
                await_bytes(near, r_near)

            send(near, near, s_fwd, r_fwd, device(k=1))

        @pl.when(k == 1)
        def _():
            await_bytes(near, r_fwd)

    def near_split():
        for j in range(3):
            high, low = halves(near[j].reshape(512, 128))
            near_b[j, :, 0:128] = high
            near_b[j, :, 128:256] = high
            near_b[j, :, 256:384] = low

    def finish(n):
        value = exc[n, pl.ds(y * 32, 32), pl.ds(pl.multiple_of(k * 128, 128), 128)] - total[n].reshape(32, 128)
        if n > 0:
            await_bytes(in_t.at[n - 1], r_t.at[n - 1])
            value = value - (terms[n - 1, z, x] + in_t[n - 1].sum(axis=0))
        new[n, y] = value
        for d in (2, 1, 3):
            send(new.at[n, y], new.at[n, y], s_g.at[n], r_g.at[n], device(y=turned("y", d)))

    def gathered(n):
        await_bytes(new.at[n, pl.ds(0, 3)], r_g.at[n])
        own = pl.ds(pl.multiple_of(k * 128, 128), 128)
        if n < 3:
            value = new[n].reshape(128, 128)
            high, low = halves(value)
            new_b[n, 0:128] = high
            new_b[n, 128:256] = low
            new_b[n, 256:384] = high
            product = dot(near_b[0], new_b[n])
            if n > 0:
                product = product + terms[n].reshape(512, 128)
            terms[n] = product.reshape(RING, RING, 32, 128)
            for dz in (2, 1, 3, 0):
                for dx in (2, 1, 3, 0):
                    if dz or dx:
                        tz, tx = turned("z", dz), turned("x", dx)
                        send(
                            terms.at[n, tz, tx], in_t.at[n, RING * dz + dx - 1],
                            s_t.at[n], r_t.at[n], device(z=tz, x=tx),
                        )
        o_ref[n, :, own] = new[n].reshape(128, 128)
        send(o_ref.at[n, :, own], o_ref.at[n, :, own], s_o.at[n], r_o.at[n], device(k=other))
        if n < 2:
            for m in range(n + 1, 3):
                product = dot(near_b[m - n], new_b[n])
                if n > 0:
                    product = product + terms[m].reshape(512, 128)
                terms[m] = product.reshape(RING, RING, 32, 128)

    at(11, near_pass)
    at(14, near_split)
    time = SUB * 3 + 1 + LAG_EXCH + LAG_ONE + LAG_TWO + LAG_THREE
    for n in range(4):
        at(time, lambda n=n: finish(n))
        time += LAG_GATHER
        at(time, lambda n=n: gathered(n))
        time += LAG_SCATTER

    def build(t):
        def rows_of(i, carry):
            for u in range(8):
                columns = pl.ds(u * 128, 128)
                even = mats[t, 2 * u, i].reshape(32, 128)
                odd = mats[t, 2 * u + 1, i].reshape(32, 128)
                top = pl.ds(pl.multiple_of(i * 32, 32), 32)
                low = pl.ds(pl.multiple_of(512 + i * 32, 32), 32)
                both[0, top, columns], both[0, low, columns] = halves(even + odd)
                both[1, top, columns], both[1, low, columns] = halves(odd)
                both[2, top, columns], both[2, low, columns] = halves(even)
            return carry

        lax.fori_loop(0, 16, rows_of, 0)

    def product(kind, pair):
        depth = pl.ds((1 - pair) * 128, 1024)
        stacked = dot(both[kind], xh[kind, depth])
        return stacked[:512] + stacked[512:] + dot(both[kind, 0:512], xl[kind, depth])

    def store(s, n, value):
        for half in range(2):
            part[s, n, half] = value[:, half * 128 : half * 128 + 128].reshape(RING, RING, RING, 8, 128)

    def run(time):
        for act in events.pop(time, []):
            act()

    for s in range(SLOTS):
        pair, t = s // 4, s % 4
        if pair == 0:
            load_a[t].wait()
        if s == 3:
            load_e.wait()
        build(t)
        first[...] = product(0, pair)
        run(SUB * s)
        store(s, 0, first[...] + product(1, pair))
        run(SUB * s + 1)
        if s == 0:
            @pl.when(lag > 0)
            def _():
                await_bytes(ext.at[2], r_carry.at[0])
            set_block(2, 1)
        if s == 4:
            pass
        store(s, 1, first[...] + product(2, pair))
        run(SUB * s + 2)
        if s == 2:
            @pl.when(lag > 0)
            def _():
                await_bytes(ext.at[pl.ds(0, 2)], r_carry.at[1])
            for kind in range(3):
                set_block(kind, 0)

    for time in sorted(events):
        run(time)

    for n in range(4):
        await_bytes(o_ref.at[n, :, pl.ds(0, 128)], r_o.at[n])
        await_bytes(o_ref.at[n, :, pl.ds(0, 128)], s_o.at[n])
        await_bytes(new.at[n, pl.ds(0, 3)], s_g.at[n])
    for n in range(3):
        await_bytes(in_t.at[n], s_t.at[n])
    await_bytes(swap, s_swap)
    await_bytes(in1, s1)
    await_bytes(in2, s2)
    await_bytes(in3, s3)

    @pl.when(lag < 7)
    def _():
        await_bytes(ext.at[2], s_carry.at[0])
        await_bytes(ext.at[pl.ds(0, 2)], s_carry.at[1])

    @pl.when(lag == 0)
    def _():
        for _i in range(3):
            await_bytes(near, s_near)

    @pl.when(k == 0)
    def _():
        await_bytes(near, s_fwd)


def local(lag_matrices, history, excitation):
    DMA = pltpu.SemaphoreType.DMA
    return pl.pallas_call(
        kernel,
        out_shape=jax.ShapeDtypeStruct((4, 128, 256), f32),
        in_specs=[pl.BlockSpec(memory_space=pl.ANY)] * 3,
        out_specs=pl.BlockSpec(memory_space=pltpu.VMEM),
        scratch_shapes=[
            pltpu.VMEM((4, 16, 16, 4, 8, 128), f32),
            pltpu.VMEM((19, 128, 256), f32),
            pltpu.VMEM((3, 1152, 256), bf),
            pltpu.VMEM((3, 1152, 256), bf),
            pltpu.VMEM((3, 1024, 1024), bf),
            pltpu.VMEM((512, 256), f32),
            pltpu.VMEM((SLOTS, 2, 2, 4, 4, 4, 8, 128), f32),
            pltpu.VMEM((SLOTS, 2, 4, 4, 4, 8, 128), f32),
            pltpu.VMEM((SLOTS, 2, 3, 4, 4, 8, 128), f32),
            pltpu.VMEM((SLOTS, 2, 4, 4, 8, 128), f32),
            pltpu.VMEM((SLOTS, 2, 3, 4, 8, 128), f32),
            pltpu.VMEM((SLOTS, 2, 4, 8, 128), f32),
            pltpu.VMEM((SLOTS, 2, 3, 8, 128), f32),
            pltpu.VMEM((4, 4, 8, 128), f32),
            pltpu.VMEM((3, 16, 32, 128), f32),
            pltpu.VMEM((3, 512, 384), bf),
            pltpu.VMEM((3, 4, 4, 32, 128), f32),
            pltpu.VMEM((3, 15, 32, 128), f32),
            pltpu.VMEM((4, 4, 32, 128), f32),
            pltpu.VMEM((3, 384, 128), bf),
            pltpu.VMEM((4, 128, 256), f32),
            DMA((4,)), DMA((3,)), DMA((2,)), DMA((2,)), DMA, DMA, DMA, DMA,
            DMA, DMA((SLOTS, 2)), DMA, DMA((SLOTS, 2)), DMA, DMA((SLOTS, 2)), DMA, DMA((SLOTS, 2)),
            DMA((3,)), DMA((3,)), DMA((4,)), DMA((4,)), DMA((4,)), DMA((4,)),
        ],
        compiler_params=pltpu.CompilerParams(
            collective_id=0, has_side_effects=True, vmem_limit_bytes=66_000_000
        ),
    )(lag_matrices.reshape(16, 16, 4, 32, 128), history, excitation)


def solution(mesh):
    return jax.shard_map(
        local,
        mesh=mesh,
        in_specs=(P("lag", None, "col"), P("lag", "col", None), P(None, "col", None)),
        out_specs=P(None, "col", None),
        check_vma=False,
    )
```

time: 298 us -> 112 us (0.38)
  blocking collectives: 126 us -> 0 us
  Pallas kernels: 0 us -> 110 us
  matrix products: 67.4 us -> 0 us
  waiting for transfers between devices: 46.8 us -> 0 us
  starting transfers between devices: 27 us -> 0 us
  local copies, waits for them, and re-layouts: 18.9 us -> 1.87 us
  other arithmetic: 10.8 us -> 0 us
    all_to_all x4 -> x0, blocking collectives: 126 us -> none  [summed_on_arrival(): lax.all_to_all(pieces, axis, split_axis=0, concat_axis=0, tiled=True)]
    pallas_call x0 -> x1, Pallas kernels: none -> 110 us  [local(): pl.pallas_call(kernel, out_shape=jax.ShapeDtypeStruct((4, 128, 256), f32)...]
    dot_general x4 -> x0, matrix products: 67.4 us -> none  [apply_lags(): jnp.einsum('jab,jbs->as', matrices, sources, precision=lax.Precision.HIGH...]
    all_to_all x4 -> x0, waiting for transfers between devices: 46.8 us -> none  [sent_to_all(): return lax.all_to_all(copies, axis, split_axis=0, concat_axis=0, tiled=True)]
    all_to_all x4 -> x0, starting transfers between devices: 23.5 us -> none  [sent_to_all(): return lax.all_to_all(copies, axis, split_axis=0, concat_axis=0, tiled=True)]
    reduce_sum x8 -> x0, other arithmetic: 5.82 us -> none  [the longest x4 3.64 us: summed_on_arrival(): return arrived.sum(axis=0)]
    unnamed x15 -> x1, local copies, waits for them, and re-layouts: 6.97 us -> 1.87 us
    broadcast_in_dim x4 -> x0, local copies, waits for them, and re-layouts: 4.32 us -> none  [sent_to_all(): copies = jnp.broadcast_to(value, (lax.axis_size(axis), *value.shape))]
  transfers between devices with their start and end apart: 5 -> 0, of which waited for: 4 -> 0; matrix products, arithmetic and copies ran while one was open for 4% -> 0% of each run, Pallas kernels for 0% -> 0%
where the time goes in v1:
time: 112 us
  Pallas kernels  110 us (98%)
  local copies, waits for them, and re-layouts  1.87 us (2%)
    pallas_call x1, Pallas kernels, local(): pl.pallas_call(kernel, out_shape=jax.ShapeDtypeStruct((4, 128, 256), f32)...  110 us

profile of v1, /device:TPU:1, one launch (start us, length us, event | category | flops | bytes accessed | tf_op | source)
XLA Modules:
  0.0 112.0 jit_solution(9958240276323812006)
XLA Ops:
  0.0 110.2 %shard_map.37 = f32[4,128,256]{2,1,0:T(8,128)} custom-call(f32[16,16,4,32,128]{4,3,2,1,0:T(8,128)} %bitcast.1, f32[16,128,256]{2,1,0:T(8,128)} %h_ref.1, f32[4,128,256]{2,1,0:T(8,128)} %e_ref.1), custom_call_target="tpu_custom_call" | custom-call | tf_op jit(solution)/shard_map/pallas_call | solution.py:337
  110.2 1.9 %copy.5 = f32[4,128,256]{2,1,0:T(8,128)} copy(f32[4,128,256]{2,1,0:T(8,128)} %shard_map.37) | data formatting | bytes 1048576

commit v2 on v1

v2 whole, which is shorter than its diff:
```python
import jax
import jax.numpy as jnp
from jax import lax
from jax.experimental import pallas as pl
from jax.experimental.pallas import tpu as pltpu
from jax.sharding import PartitionSpec as P

MESH = pl.DeviceIdType.MESH
bf, f32 = jnp.bfloat16, jnp.float32

RING = 4
SLOTS = 8
LAG_ONE, LAG_TWO, LAG_THREE = 2, 2, 2
WAIT_ONE, WAIT_TWO, WAIT_THREE = 4.0, 3.5, 3.0
SEND, PASS, SPLIT = (0, 2, 4), (5, 9, 11), (6, 10, 12)
WAIT_GATHER, WAIT_SCATTER, AHEAD = 2.5, 4.0, 0.5


def halves(value):
    high = value.astype(bf)
    return high, (value - high.astype(f32)).astype(bf)


def dot(a, b):
    return jnp.dot(a, b, preferred_element_type=f32)


def kernel(
    a_ref, h_ref, e_ref, o_ref,
    mats, ext, xh, xl, both, first, part, swap,
    in1, sum1, in2, sum2, in3, total,
    near, near_b, terms, in_t, new, new_b, exc, came, came_b,
    s_mat, s_loc, s_carry, r_carry, s_near, r_near, s_fwd, r_fwd,
    s_swap, r_swap, s1, r1, s2, r2, s3, r3, s_t, r_t, s_g, r_g, s_o, r_o,
):
    lag, col = lax.axis_index("lag"), lax.axis_index("col")
    y, k = lag // 2, lag % 2
    z, x = col // RING, col % RING
    pos = {"x": x, "y": y, "z": z}
    other = 1 - k

    def device(**moved):
        at = {**pos, "k": k, **moved}
        return (at["y"] * 2 + at["k"], at["z"] * RING + at["x"])

    def turned(axis, steps):
        return lax.rem(pos[axis] + steps, RING)

    def send(src, dst, s_sem, r_sem, target):
        pltpu.make_async_remote_copy(
            src_ref=src, dst_ref=dst, send_sem=s_sem, recv_sem=r_sem,
            device_id=target, device_id_type=MESH,
        ).start()

    def await_bytes(ref, sem):
        pltpu.make_async_copy(ref, ref, sem).wait()

    load_h = pltpu.make_async_copy(h_ref, ext.at[pl.ds(3, 16)], s_loc.at[0])
    load_h.start()

    barrier = pltpu.get_barrier_semaphore()
    cross = (lax.rem(y + jnp.where(k == 1, 1, RING - 1), RING) * 2 + other, col)
    peers = [device(k=other), cross]
    peers += [device(y=turned("y", d)) for d in range(1, RING)]
    peers += [
        device(z=turned("z", dz), x=turned("x", dx))
        for dz in range(RING) for dx in range(RING) if dz or dx
    ]
    for peer in peers:
        pl.semaphore_signal(barrier, inc=1, device_id=peer, device_id_type=MESH)

    for t in range(4):
        pltpu.make_async_copy(a_ref.at[:, :, :, pl.ds(8 * t, 8)], mats.at[t], s_mat.at[t]).start()
    load_e = pltpu.make_async_copy(e_ref, exc, s_loc.at[1])
    load_e.start()

    ext[0:3] = jnp.zeros((3, 128, 256), f32)
    load_h.wait()

    def set_block(kind, u):
        def piece(i, carry):
            part_rows = pl.ds(pl.multiple_of(32 * i, 32), 32)
            base = ext[1 + 2 * u, part_rows]
            if kind == 0:
                value = base
            else:
                value = ext[(2 + 2 * u) if kind == 1 else 2 * u, part_rows] - base
            rows = pl.ds(pl.multiple_of(u * 128 + 32 * i, 32), 32)
            xh[kind, rows], xl[kind, rows] = halves(value)
            return carry

        lax.fori_loop(0, 4, piece, 0)

    def set_blocks(u, carry):
        for kind in range(3):
            set_block(kind, u)
        return carry

    lax.fori_loop(1, 9, set_blocks, 0)

    def greet():
        pl.semaphore_wait(barrier, len(peers))

        @pl.when(lag < 7)
        def _():
            after = (lag + 1, col)
            send(h_ref.at[15], came.at[2], s_carry.at[0], r_carry.at[0], after)
            send(h_ref.at[pl.ds(13, 2)], came.at[pl.ds(0, 2)], s_carry.at[1], r_carry.at[1], after)

        @pl.when(lag == 0)
        def _():
            came[...] = jnp.zeros((3, 128, 256), f32)
            pltpu.make_async_copy(a_ref.at[pl.ds(0, 3), :, 0], near, s_loc.at[2]).start()

    def near_send(j):
        @pl.when(lag == 0)
        def _():
            for d in (1, 3, 2):
                send(a_ref.at[j, :, d], near.at[j], s_near, r_near.at[j], device(y=d))

    orders = ("xzy", "zxy")

    def scatter(s, n, stage, size, src, dst, s_sem, r_sem):
        axis = orders[n][stage]
        for d in (2, 1, 3):
            to = turned(axis, d)
            send(src.at[pl.ds(to * size, size)], dst.at[d - 1], s_sem, r_sem, device(**{axis: to}))

    def swap_send(s):
        send(part.at[s, other], swap.at[s], s_swap, r_swap.at[s], device(k=other))

    def exchange(s):
        await_bytes(swap.at[s], r_swap.at[s])
        for n in range(2):
            part[s, k, n] += swap[s, n]
        for n in range(2):
            scatter(s, n, 0, 16, part.at[s, k, n], in1.at[s, n], s1, r1.at[s])

    def own(s, n, stage, size):
        return pl.ds(pos[orders[n][stage]] * size, size)

    def one(s):
        await_bytes(in1.at[s], r1.at[s])
        for n in range(2):
            sum1[s, n] = (part[s, k, n, own(s, n, 0, 16)] + in1[s, n, 0]) + (in1[s, n, 1] + in1[s, n, 2])
        for n in range(2):
            scatter(s, n, 1, 4, sum1.at[s, n], in2.at[s, n], s2, r2.at[s])

    def two(s):
        await_bytes(in2.at[s], r2.at[s])
        for n in range(2):
            sum2[s, n] = (sum1[s, n, own(s, n, 1, 4)] + in2[s, n, 0]) + (in2[s, n, 1] + in2[s, n, 2])
        for n in range(2):
            scatter(s, n, 2, 1, sum2.at[s, n], in3.at[s, n], s3, r3.at[s])

    def three(s):
        await_bytes(in3.at[s], r3.at[s])
        for n in range(2):
            value = (sum2[s, n, own(s, n, 2, 1)] + in3[s, n, 0]) + (in3[s, n, 1] + in3[s, n, 2])
            total[2 * (s // 4) + n, lax.rem(s, 4)] = value[0]

    def near_pass(j):
        @pl.when(k == 0)
        def _():
            if j == 0:
                @pl.when(y == 0)
                def _():
                    await_bytes(near, s_loc.at[2])

            @pl.when(y > 0)
            def _():
                await_bytes(near.at[j], r_near.at[j])

            send(near.at[j], near.at[j], s_fwd, r_fwd.at[j], device(k=1))

    def near_split(j):
        @pl.when(k == 1)
        def _():
            await_bytes(near.at[j], r_fwd.at[j])

        def piece(i, carry):
            rows = pl.ds(pl.multiple_of(32 * i, 32), 32)
            high, low = halves(near[j, i])
            near_b[j, rows, 0:128] = high
            near_b[j, rows, 128:256] = high
            near_b[j, rows, 256:384] = low
            return carry

        lax.fori_loop(0, 16, piece, 0)

    def finish(n):
        if n == 0:
            load_e.wait()
        value = exc[n, pl.ds(y * 32, 32), pl.ds(pl.multiple_of(k * 128, 128), 128)] - total[n].reshape(32, 128)
        if n > 0:
            await_bytes(in_t.at[n - 1], r_t.at[n - 1])
            value = value - (terms[n - 1, z, x] + in_t[n - 1].sum(axis=0))
        new[n, y] = value
        for d in (2, 1, 3):
            send(new.at[n, y], new.at[n, y], s_g.at[n], r_g.at[n], device(y=turned("y", d)))

    def add_term(m, n):
        term = dot(near_b[m - n], new_b[n])
        if n > 0:
            term = term + terms[m].reshape(512, 128)
        terms[m] = term.reshape(RING, RING, 32, 128)

    def gathered(n):
        await_bytes(new.at[n, pl.ds(0, 3)], r_g.at[n])
        own = pl.ds(pl.multiple_of(k * 128, 128), 128)
        if n < 3:
            high, low = halves(new[n].reshape(128, 128))
            new_b[n, 0:128] = high
            new_b[n, 128:256] = low
            new_b[n, 256:384] = high
            add_term(n, n)
            for dz in (2, 1, 3, 0):
                for dx in (2, 1, 3, 0):
                    if dz or dx:
                        tz, tx = turned("z", dz), turned("x", dx)
                        send(
                            terms.at[n, tz, tx], in_t.at[n, RING * dz + dx - 1],
                            s_t.at[n], r_t.at[n], device(z=tz, x=tx),
                        )
        o_ref[n, :, own] = new[n].reshape(128, 128)
        send(o_ref.at[n, :, own], o_ref.at[n, :, own], s_o.at[n], r_o.at[n], device(k=other))

    def ahead(n):
        for m in range(n + 1, 3):
            add_term(m, n)

    def build(t):
        for i in range(0, 64, 2):
            top, low = pl.ds(8 * i, 16), pl.ds(512 + 8 * i, 16)
            pair_of = (i // RING, pl.ds(i % RING, 2))
            for u in range(8):
                columns = pl.ds(u * 128, 128)
                even = mats[(t, 2 * u, *pair_of)].reshape(16, 128)
                odd = mats[(t, 2 * u + 1, *pair_of)].reshape(16, 128)
                both[0, top, columns], both[0, low, columns] = halves(even + odd)
                both[1, top, columns], both[1, low, columns] = halves(odd)
                both[2, top, columns], both[2, low, columns] = halves(even)

    def product(kind, pair):
        depth = pl.ds(pl.multiple_of((1 - pair) * 128, 128), 1024)
        stacked = dot(both[kind], xh[kind, depth])
        return stacked[:512] + stacked[512:] + dot(both[kind, 0:512], xl[kind, depth])

    def store(s, n, value, add=False):
        step_x, step_y, step_z = ((16, 1, 4), (4, 1, 16))[n]
        for unit in range(64):
            to = (unit // 16) * step_z + (unit // 4 % 4) * step_x + (unit % 4) * step_y
            for half in range(2):
                piece = value[8 * unit : 8 * unit + 8, half * 128 : half * 128 + 128]
                if add:
                    piece = piece + part[s, half, n, to]
                part[s, half, n, to] = piece

    def late(s):
        for i in range(0, 64, 2):
            high, low = halves(mats[s, 0, i // RING, pl.ds(i % RING, 2)].reshape(16, 128))
            rows = pl.ds(8 * i, 16)
            first[rows, 0:128] = high
            first[rows, 128:256] = high
            first[rows, 256:384] = low
        store(s, 1, dot(first[...], came_b[...]), True)

    def first_came():
        @pl.when(lag > 0)
        def _():
            await_bytes(came.at[2], r_carry.at[0])

        high, low = halves(came[2])
        came_b[0:128] = high
        came_b[128:256] = low
        came_b[256:384] = high
        ext[2] = came[2]
        set_block(2, 1)
        for s in range(2):
            late(s)
            swap_send(s)

    def rest_came():
        @pl.when(lag > 0)
        def _():
            await_bytes(came.at[pl.ds(0, 2)], r_carry.at[1])

        ext[0:2] = came[0:2]
        for kind in range(3):
            set_block(kind, 0)

    acts = ((exchange, 1), (one, 1 + LAG_ONE), (two, 1 + LAG_ONE + LAG_TWO), (three, 1 + LAG_ONE + LAG_TWO + LAG_THREE))

    def when(s, value, act, *args):
        pl.when(s == value)(lambda: act(*args))

    def slot(s, carry):
        pair, t = s // 4, lax.rem(s, 4)

        @pl.when(pair == 0)
        def _():
            await_bytes(mats.at[t], s_mat.at[t])

        build(t)
        base = product(0, pair)
        store(s, 0, base + product(1, pair))
        store(s, 1, base + product(2, pair))
        when(s, 0, greet)
        when(s, 1, first_came)
        pl.when(s > 1)(lambda: swap_send(s))
        when(s, 2, exchange, 0)
        for act, lag_ in acts[::-1]:
            pl.when(s >= lag_ + (act is exchange))(lambda act=act, lag_=lag_: act(s - lag_))
        when(s, 3, rest_came)
        for j in range(3):
            when(s, SEND[j], near_send, j)
            when(s, PASS[j], near_pass, j)
            when(s, SPLIT[j], near_split, j)
        return carry

    lax.fori_loop(0, SLOTS, slot, 0)

    left = []
    for s in range(SLOTS):
        done = 0.0
        for (act, lag_), wait in zip(acts, (1.5, WAIT_ONE, WAIT_TWO, WAIT_THREE)):
            if s + lag_ < SLOTS:
                done = 3.5 * (s + lag_ - SLOTS + 1)
            else:
                done = max(done + wait, 0.1 + 0.01 * s)
                left.append((done, act, s))
                if act is three and s == 3:
                    begin = done
    begin = 0.05 if 3 + acts[-1][1] < SLOTS else begin + 0.001
    time = begin
    for n in range(4):
        left.append((time, finish, n))
        time += WAIT_GATHER
        left.append((time, gathered, n))
        time += WAIT_SCATTER
        if n < 2:
            left.append((time + AHEAD, ahead, n))
    for j in range(3):
        for times, act in ((PASS, near_pass), (SPLIT, near_split)):
            if times[j] >= SLOTS:
                left.append((times[j] - SLOTS + 0.001, act, j))
    for _, act, value in sorted(left, key=lambda item: item[0]):
        act(value)

    for n in range(4):
        await_bytes(o_ref.at[n, :, pl.ds(0, 128)], r_o.at[n])
        await_bytes(o_ref.at[n, :, pl.ds(0, 128)], s_o.at[n])
        await_bytes(new.at[n, pl.ds(0, 3)], s_g.at[n])
    for n in range(3):
        await_bytes(in_t.at[n], s_t.at[n])
    await_bytes(swap, s_swap)
    await_bytes(in1, s1)
    await_bytes(in2, s2)
    await_bytes(in3, s3)

    @pl.when(lag < 7)
    def _():
        await_bytes(came.at[2], s_carry.at[0])
        await_bytes(came.at[pl.ds(0, 2)], s_carry.at[1])

    @pl.when(lag == 0)
    def _():
        for _i in range(3):
            await_bytes(near, s_near)

    @pl.when(k == 0)
    def _():
        await_bytes(near, s_fwd)


def local(lag_matrices, history, excitation):
    DMA = pltpu.SemaphoreType.DMA
    return pl.pallas_call(
        kernel,
        out_shape=jax.ShapeDtypeStruct((4, 128, 256), f32),
        in_specs=[pl.BlockSpec(memory_space=pl.ANY)] * 3,
        out_specs=pl.BlockSpec(memory_space=pltpu.VMEM),
        scratch_shapes=[
            pltpu.VMEM((4, 16, 16, 4, 8, 128), f32),
            pltpu.VMEM((19, 128, 256), f32),
            pltpu.VMEM((3, 1152, 256), bf),
            pltpu.VMEM((3, 1152, 256), bf),
            pltpu.VMEM((3, 1024, 1024), bf),
            pltpu.VMEM((512, 384), bf),
            pltpu.VMEM((SLOTS, 2, 2, 64, 8, 128), f32),
            pltpu.VMEM((SLOTS, 2, 64, 8, 128), f32),
            pltpu.VMEM((SLOTS, 2, 3, 16, 8, 128), f32),
            pltpu.VMEM((SLOTS, 2, 16, 8, 128), f32),
            pltpu.VMEM((SLOTS, 2, 3, 4, 8, 128), f32),
            pltpu.VMEM((SLOTS, 2, 4, 8, 128), f32),
            pltpu.VMEM((SLOTS, 2, 3, 1, 8, 128), f32),
            pltpu.VMEM((4, 4, 8, 128), f32),
            pltpu.VMEM((3, 16, 32, 128), f32),
            pltpu.VMEM((3, 512, 384), bf),
            pltpu.VMEM((3, 4, 4, 32, 128), f32),
            pltpu.VMEM((3, 15, 32, 128), f32),
            pltpu.VMEM((4, 4, 32, 128), f32),
            pltpu.VMEM((3, 384, 128), bf),
            pltpu.VMEM((4, 128, 256), f32),
            pltpu.VMEM((3, 128, 256), f32),
            pltpu.VMEM((384, 256), bf),
            DMA((4,)), DMA((3,)), DMA((2,)), DMA((2,)), DMA, DMA((3,)), DMA, DMA((3,)),
            DMA, DMA((SLOTS,)), DMA, DMA((SLOTS,)), DMA, DMA((SLOTS,)), DMA, DMA((SLOTS,)),
            DMA((3,)), DMA((3,)), DMA((4,)), DMA((4,)), DMA((4,)), DMA((4,)),
        ],
        compiler_params=pltpu.CompilerParams(
            collective_id=0, has_side_effects=True, vmem_limit_bytes=66_000_000
        ),
    )(lag_matrices.reshape(16, 16, 4, 32, 128), history, excitation)


def solution(mesh):
    return jax.shard_map(
        local,
        mesh=mesh,
        in_specs=(P("lag", None, "col"), P("lag", "col", None), P(None, "col", None)),
        out_specs=P(None, "col", None),
        check_vma=False,
    )
```

time: 112 us -> 79.6 us (0.71)
  Pallas kernels: 110 us -> 77.6 us
    pallas_call x1, Pallas kernels: 110 us -> 77.6 us  [local(): pl.pallas_call(kernel, out_shape=jax.ShapeDtypeStruct((4, 128, 256), f32)...]
where the time goes in v2:
time: 79.6 us; the launch traced here: 79.5 us
  Pallas kernels  77.6 us (97%)
  local copies, waits for them, and re-layouts  1.87 us (2%)
    pallas_call x1, Pallas kernels, local(): pl.pallas_call(kernel, out_shape=jax.ShapeDtypeStruct((4, 128, 256), f32)...  77.6 us
    unnamed x1, local copies, waits for them, and re-layouts  1.87 us

profile of v2, /device:TPU:1, one launch (start us, length us, event | category | flops | bytes accessed | tf_op | source)
XLA Modules:
  0.0 79.5 jit_solution(2149890872725787433)
XLA Ops:
  0.0 77.6 %shard_map.37 = f32[4,128,256]{2,1,0:T(8,128)} custom-call(f32[16,16,4,32,128]{4,3,2,1,0:T(8,128)} %bitcast.1, f32[16,128,256]{2,1,0:T(8,128)} %h_ref.1, f32[4,128,256]{2,1,0:T(8,128)} %e_ref.1), custom_call_target="tpu_custom_call" | custom-call | tf_op jit(solution)/shard_map/pallas_call | solution.py:378
  77.6 1.9 %copy.5 = f32[4,128,256]{2,1,0:T(8,128)} copy(f32[4,128,256]{2,1,0:T(8,128)} %shard_map.37) | data formatting | bytes 1048576

commit v3 on v2

--- a/solution.py
+++ b/solution.py
@@ -276,9 +276,8 @@
         came_b[256:384] = high
         ext[2] = came[2]
         set_block(2, 1)
-        for s in range(2):
-            late(s)
-            swap_send(s)
+        late(0)
+        swap_send(0)
 
     def rest_came():
         @pl.when(lag > 0)
@@ -305,12 +304,10 @@
         base = product(0, pair)
         store(s, 0, base + product(1, pair))
         store(s, 1, base + product(2, pair))
-        when(s, 0, greet)
-        when(s, 1, first_came)
-        pl.when(s > 1)(lambda: swap_send(s))
-        when(s, 2, exchange, 0)
+        when(s, 0, first_came)
+        pl.when(s > 0)(lambda: swap_send(s))
         for act, lag_ in acts[::-1]:
-            pl.when(s >= lag_ + (act is exchange))(lambda act=act, lag_=lag_: act(s - lag_))
+            pl.when(s >= lag_)(lambda act=act, lag_=lag_: act(s - lag_))
         when(s, 3, rest_came)
         for j in range(3):
             when(s, SEND[j], near_send, j)
@@ -318,6 +315,7 @@
             when(s, SPLIT[j], near_split, j)
         return carry
 
+    greet()
     lax.fori_loop(0, SLOTS, slot, 0)
 
     left = []

time: 79.6 us -> 76.6 us (0.962)
  Pallas kernels: 77.6 us -> 74.6 us
    pallas_call x1, Pallas kernels: 77.6 us -> 74.6 us  [local(): pl.pallas_call(kernel, out_shape=jax.ShapeDtypeStruct((4, 128, 256), f32)...]
where the time goes in v3:
time: 76.6 us; the launch traced here: 76.5 us
  Pallas kernels  74.6 us (97%)
  local copies, waits for them, and re-layouts  1.87 us (2%)
    pallas_call x1, Pallas kernels, local(): pl.pallas_call(kernel, out_shape=jax.ShapeDtypeStruct((4, 128, 256), f32)...  74.6 us
    unnamed x1, local copies, waits for them, and re-layouts  1.87 us

profile of v3, /device:TPU:1, one launch (start us, length us, event | category | flops | bytes accessed | tf_op | source)
XLA Modules:
  0.0 76.5 jit_solution(15890946066939731574)
XLA Ops:
  0.0 74.6 %shard_map.37 = f32[4,128,256]{2,1,0:T(8,128)} custom-call(f32[16,16,4,32,128]{4,3,2,1,0:T(8,128)} %bitcast.1, f32[16,128,256]{2,1,0:T(8,128)} %h_ref.1, f32[4,128,256]{2,1,0:T(8,128)} %e_ref.1), custom_call_target="tpu_custom_call" | custom-call | tf_op jit(solution)/shard_map/pallas_call | solution.py:376
  74.6 1.9 %copy.5 = f32[4,128,256]{2,1,0:T(8,128)} copy(f32[4,128,256]{2,1,0:T(8,128)} %shard_map.37) | data formatting | bytes 1048576
